TPU v7x, 32 devices: a whole 2x2x4 slice. The times are simulated.
32 devices in a mesh: slot: 4 (over y, x), seq: 2 (over core), blk: 4 (over z).
Axes of the slice: x: 2, y: 2, z: 4, core: 2. Of those that a mesh axis runs over, the one named last changes fastest.
Arguments:
- tokens: bfloat16 [4, 1024, 2048], P('slot', ('blk', 'seq')), may hold values from -6 to 6
- out_grad: bfloat16 [4, 1024, 2048], P('slot', ('blk', 'seq')), may hold values from -6 to 6
- lengths: int32 [4], P('slot'), may hold values from 256 to 1024, as said below
- attn_gain: bfloat16 [2048], P(('slot', 'blk')), may hold values from 0.099609375 to 1.8984375
- w_query: bfloat16 [2048, 2048], P(('slot', 'blk'), 'seq'), may hold values from -0.125 to 0.125
- w_key: bfloat16 [2048, 2048], P(('slot', 'blk'), 'seq'), may hold values from -0.125 to 0.125
- w_value: bfloat16 [2048, 2048], P(('slot', 'blk'), 'seq'), may hold values from -0.125 to 0.125
- output_weight: bfloat16 [2048, 2048], P(('slot', 'blk'), 'seq'), may hold values from -1 to 1
- mlp_gain: bfloat16 [2048], P(('slot', 'blk')), may hold values from 0.099609375 to 1.8984375
- gate_weight: bfloat16 [2048, 8192], P(('slot', 'blk'), 'seq'), may hold values from -0.125 to 0.125
- up_weight: bfloat16 [2048, 8192], P(('slot', 'blk'), 'seq'), may hold values from -0.125 to 0.125
- down_weight: bfloat16 [2048, 8192], P(('slot', 'blk'), 'seq'), may hold values from -0.0625 to 0.0625
Outputs:
- layer_out: bfloat16 [4, 1024, 2048], P('slot', ('blk', 'seq'))
- grad_tokens: float32 [4, 1024, 2048], P('slot', ('blk', 'seq'))
- grad_attn_gain: float32 [2048], P(('slot', 'blk'))
- grad_w_query: float32 [2048, 2048], P(('slot', 'blk'), 'seq')
- grad_w_key: float32 [2048, 2048], P(('slot', 'blk'), 'seq')
- grad_w_value: float32 [2048, 2048], P(('slot', 'blk'), 'seq')
- grad_w_output: float32 [2048, 2048], P(('slot', 'blk'), 'seq')
- grad_mlp_gain: float32 [2048], P(('slot', 'blk'))
- grad_w_gate: float32 [2048, 8192], P(('slot', 'blk'), 'seq')
- grad_w_up: float32 [2048, 8192], P(('slot', 'blk'), 'seq')
- grad_w_down: float32 [2048, 8192], P(('slot', 'blk'), 'seq')
Inputs may be any that keep to these rules, and one draw needn't show every extreme that they name: `lengths`: the valid tokens of a slot are its first ones; at least one slot is full.
All inputs are finite; a program needn't handle non-finite values.
Results may differ from a plain program's by a relative error of at most 0.025.
Values may be sent and summed in bfloat16 or wider, within the bound.
No kernel may reach another device: no remote copies, remote signals or barrier semaphores. Data moves between devices by JAX's collectives and lax.ppermute only.
A program may use at most 192 MiB of HBM per device.

v0:
```python
from functools import partial
import jax
import jax.numpy as jnp
from jax import lax
from jax.sharding import PartitionSpec as P

HEADS = 32
HEAD_DIM = 64
EPSILON = 1e-05
ROPE_BASE = 130000.0


def from_behind(value, axis, steps):
    count = lax.axis_size(axis)
    first, last = (max(0, -steps), min(count, count - steps))
    return lax.ppermute(value, axis, [(source, source + steps) for source in range(first, last)])


def from_behind_2(array, axis, by):
    peers = lax.axis_size(axis)
    return lax.ppermute(array, axis, [(i, (i + by) % peers) for i in range(peers)])


def rope_tables(positions, head_size):
    half_size = head_size // 2
    frequency = ROPE_BASE ** (-jnp.arange(half_size, dtype=jnp.float32) * 2.0 / head_size)
    angles = positions.astype(jnp.float32)[:, None] * frequency[None, :]
    return (jnp.cos(angles), jnp.sin(angles))


def rotate(vectors, cosine, sine_tab):
    half_size = vectors.shape[-1] // 2
    first_half = vectors[..., :half_size]
    second_half = vectors[..., half_size:]
    cos_wide = cosine[:, None, :]
    sin_wide = sine_tab[:, None, :]
    return jnp.concatenate(
        [
            first_half * cos_wide - second_half * sin_wide,
            second_half * cos_wide + first_half * sin_wide,
        ],
        axis=-1,
    )


def norm_rows(input_rows_packed, gain_row):
    inverse = lax.rsqrt(
        jnp.mean(input_rows_packed * input_rows_packed, axis=-1, keepdims=True) + EPSILON
    )
    return (input_rows_packed * inverse * gain_row, inverse)


def norm_back(input_rows_packed, inverse, gain_row, upstream):
    scaled = upstream * gain_row
    normed = input_rows_packed * inverse
    grad_in = inverse * (scaled - normed * jnp.mean(scaled * normed, axis=-1, keepdims=True))
    return (grad_in, jnp.sum(upstream * normed, axis=0))


def matmul(left, right):
    return jnp.dot(left, right, preferred_element_type=jnp.float32)


def over_rows(left, right):
    return lax.dot_general(
        left, right, (((0,), (0,)), ((), ())), preferred_element_type=jnp.float32
    )


def over_cols(left, right):
    return lax.dot_general(
        left, right, (((1,), (1,)), ((), ())), preferred_element_type=jnp.float32
    )


def block_scores(queries, key_rows, query_pos, key_first, length, score_scale):
    key_pos = key_first + jnp.arange(key_rows.shape[0], dtype=jnp.int32)
    allowed = (key_pos[None, :] <= query_pos[:, None]) & (key_pos[None, :] < length)
    scores = (
        jnp.einsum("qhd,khd->hqk", queries, key_rows, preferred_element_type=jnp.float32)
        * score_scale
    )
    return jnp.where(allowed[None, :, :], scores, -jnp.inf)


def attend_tile(tile_item, key_rows, val_rows, key_first, length, score_scale):
    queries, query_pos, run_max, run_sum, run_out = tile_item
    scores = block_scores(queries, key_rows, query_pos, key_first, length, score_scale)
    new_max = jnp.maximum(run_max, jnp.max(scores, axis=2))
    factor = jnp.exp(run_max - new_max)
    exp_weights = jnp.exp(scores - new_max[:, :, None])
    run_sum = run_sum * factor + jnp.sum(exp_weights, axis=2)
    mixed_out = jnp.einsum(
        "hqk,khd->qhd",
        exp_weights.astype(jnp.bfloat16),
        val_rows,
        preferred_element_type=jnp.float32,
    )
    run_out = run_out * jnp.transpose(factor)[:, :, None] + mixed_out
    return (new_max, run_sum, run_out)


def back_tile(carried, tile_item, key_rows, val_rows, key_first, length, score_scale):
    grad_keys, grad_vals = carried
    queries, query_pos, out_cot, log_sum, row_dot, grad_query = tile_item
    scores = block_scores(queries, key_rows, query_pos, key_first, length, score_scale)
    probs = jnp.exp(scores - log_sum[:, :, None])
    grad_vals = grad_vals + jnp.einsum(
        "hqk,qhd->khd", probs.astype(jnp.bfloat16), out_cot, preferred_element_type=jnp.float32
    )
    grad_weight = jnp.einsum("qhd,khd->hqk", out_cot, val_rows, preferred_element_type=jnp.float32)
    grad_scores = (probs * (grad_weight - row_dot[:, :, None])).astype(jnp.bfloat16)
    grad_query = (
        grad_query
        + jnp.einsum("hqk,khd->qhd", grad_scores, key_rows, preferred_element_type=jnp.float32)
        * score_scale
    )
    grad_keys = (
        grad_keys
        + jnp.einsum("hqk,qhd->khd", grad_scores, queries, preferred_element_type=jnp.float32)
        * score_scale
    )
    return ((grad_keys, grad_vals), grad_query)


def sum_mlp(term_gate, term_up, term_down):
    return (
        lax.psum_scatter(
            term_gate.astype(jnp.bfloat16), ("slot", "blk"), scatter_dimension=0, tiled=True
        ).astype(jnp.float32),
        lax.psum_scatter(
            term_up.astype(jnp.bfloat16), ("slot", "blk"), scatter_dimension=0, tiled=True
        ).astype(jnp.float32),
        lax.psum_scatter(
            term_down.astype(jnp.bfloat16), ("slot", "blk"), scatter_dimension=0, tiled=True
        ).astype(jnp.float32),
    )


def shards(
    tokens,
    out_grad,
    lengths,
    attn_gain,
    w_query,
    w_key,
    w_value,
    output_weight,
    mlp_gain,
    gate_weight,
    up_weight,
    down_weight,
):
    seq_count = lax.axis_size("seq")
    blk_count = lax.axis_size("blk")
    seq_rank = lax.axis_index("seq")
    blk_rank = lax.axis_index("blk")
    tok_rows = tokens.shape[1]
    block_len = tok_rows * seq_count
    local_heads = HEADS // seq_count
    local_width = local_heads * HEAD_DIM
    score_scale = HEAD_DIM ** (-0.5)
    length = lengths[0]
    block_pos = blk_rank * block_len + jnp.arange(block_len, dtype=jnp.int32)
    positions = blk_rank * block_len + seq_rank * tok_rows + jnp.arange(tok_rows, dtype=jnp.int32)
    live_rows = (positions < length)[:, None]
    input_rows_packed = tokens[0].astype(jnp.float32)
    cosine, sine_tab = rope_tables(block_pos, HEAD_DIM)
    head_shape = (block_len, local_heads, HEAD_DIM)
    tile_rows = min(512, block_len)
    tile_count = block_len // tile_rows
    tiled_shape = (tile_count, tile_rows, local_heads, HEAD_DIM)
    pos_tiles = block_pos.reshape(tile_count, tile_rows)
    (
        gain_attn,
        gain_mlp,
        full_query,
        full_key,
        full_value,
        full_output,
        full_gate,
        full_up,
        full_down,
    ) = (
        lax.all_gather(attn_gain, ("slot", "blk"), axis=0, tiled=True),
        lax.all_gather(mlp_gain, ("slot", "blk"), axis=0, tiled=True),
        lax.all_gather(w_query, ("slot", "blk"), axis=0, tiled=True),
        lax.all_gather(w_key, ("slot", "blk"), axis=0, tiled=True),
        lax.all_gather(w_value, ("slot", "blk"), axis=0, tiled=True),
        lax.all_gather(output_weight, ("slot", "blk"), axis=0, tiled=True),
        lax.all_gather(gate_weight, ("slot", "blk"), axis=0, tiled=True),
        lax.all_gather(up_weight, ("slot", "blk"), axis=0, tiled=True),
        lax.all_gather(down_weight, ("slot", "blk"), axis=0, tiled=True),
    )
    gain_attn_f = gain_attn.astype(jnp.float32)
    gain_mlp_f = gain_mlp.astype(jnp.float32)
    normed_attn, inverse_attn = norm_rows(input_rows_packed, gain_attn_f)
    hidden_after_attention = normed_attn.astype(jnp.bfloat16)
    hidden_block = lax.all_gather(hidden_after_attention, "seq", axis=0, tiled=True)
    queries = rotate(matmul(hidden_block, full_query).reshape(head_shape), cosine, sine_tab).astype(
        jnp.bfloat16
    )
    key_rows = rotate(matmul(hidden_block, full_key).reshape(head_shape), cosine, sine_tab).astype(
        jnp.bfloat16
    )
    val_rows = matmul(hidden_block, full_value).astype(jnp.bfloat16).reshape(head_shape)
    query_tiles = queries.reshape(tiled_shape)
    run_max = jnp.full((tile_count, local_heads, tile_rows), -1e30, jnp.float32)
    run_sum = jnp.zeros((tile_count, local_heads, tile_rows), jnp.float32)
    run_out = jnp.zeros(tiled_shape, jnp.float32)
    kept_blocks = []
    moving_keys, moving_vals = (key_rows, val_rows)
    for cycle_step in range(blk_count):
        key_first = (blk_rank - cycle_step) % blk_count * block_len
        kept_blocks.append((moving_keys, moving_vals, key_first))
        step_fn = partial(
            attend_tile,
            key_rows=moving_keys,
            val_rows=moving_vals,
            key_first=key_first,
            length=length,
            score_scale=score_scale,
        )
        run_max, run_sum, run_out = lax.map(
            step_fn, (query_tiles, pos_tiles, run_max, run_sum, run_out)
        )
        if cycle_step + 1 < blk_count:
            moving_keys, moving_vals = from_behind((moving_keys, moving_vals), "blk", 1)
    log_sum = run_max + jnp.log(run_sum)
    attended_tiles = (run_out / jnp.transpose(run_sum, (0, 2, 1))[:, :, :, None]).astype(
        jnp.bfloat16
    )
    attention_mixed = attended_tiles.reshape(block_len, local_width)
    residual_stream = input_rows_packed + lax.psum_scatter(
        over_cols(attention_mixed, full_output).astype(jnp.bfloat16),
        "seq",
        scatter_dimension=0,
        tiled=True,
    ).astype(jnp.float32)
    normed_mlp, inverse_mlp = norm_rows(residual_stream, gain_mlp_f)
    hidden_after_feedforward = normed_mlp.astype(jnp.bfloat16)
    mlp_block = lax.all_gather(hidden_after_feedforward, "seq", axis=0, tiled=True)
    gate_logits = matmul(mlp_block, full_gate)
    up_logits = matmul(mlp_block, full_up)
    sigmoid_gate = jax.nn.sigmoid(gate_logits)
    swiglu_product = (gate_logits * sigmoid_gate * up_logits).astype(jnp.bfloat16)
    mlp_proj = lax.psum_scatter(
        over_cols(swiglu_product, full_down).astype(jnp.bfloat16),
        "seq",
        scatter_dimension=0,
        tiled=True,
    ).astype(jnp.float32)
    block_out = jnp.where(live_rows, residual_stream + mlp_proj, 0.0)
    out_cot = jnp.where(live_rows, out_grad[0].astype(jnp.float32), 0.0)
    cot_block = lax.all_gather(out_cot.astype(jnp.bfloat16), "seq", axis=0, tiled=True)
    grad_down_term = over_rows(cot_block, swiglu_product)
    grad_act = matmul(cot_block, full_down)
    grad_gate = (
        grad_act * up_logits * sigmoid_gate * (1.0 + gate_logits * (1.0 - sigmoid_gate))
    ).astype(jnp.bfloat16)
    grad_up = (grad_act * gate_logits * sigmoid_gate).astype(jnp.bfloat16)
    grad_gate_term = over_rows(mlp_block, grad_gate)
    grad_up_term = over_rows(mlp_block, grad_up)
    grad_hidden_mlp = lax.psum_scatter(
        (over_cols(grad_gate, full_gate) + over_cols(grad_up, full_up)).astype(jnp.bfloat16),
        "seq",
        scatter_dimension=0,
        tiled=True,
    ).astype(jnp.float32)
    grad_resid_part, gain_mlp_term = norm_back(
        residual_stream, inverse_mlp, gain_mlp_f, grad_hidden_mlp
    )
    grad_resid = out_cot + grad_resid_part
    resid_block = lax.all_gather(grad_resid.astype(jnp.bfloat16), "seq", axis=0, tiled=True)
    grad_wout_term = over_rows(resid_block, attention_mixed)
    grad_attended = matmul(resid_block, full_output).astype(jnp.bfloat16)
    cot_tiles = grad_attended.reshape(tiled_shape)
    row_dot = jnp.transpose(
        jnp.sum(cot_tiles.astype(jnp.float32) * attended_tiles.astype(jnp.float32), axis=-1),
        (0, 2, 1),
    )
    grad_query = jnp.zeros(tiled_shape, jnp.float32)
    moving_grads = (jnp.zeros(head_shape, jnp.float32), jnp.zeros(head_shape, jnp.float32))
    for kept_keys, kept_vals, key_first in kept_blocks:
        back_fn = partial(
            back_tile,
            key_rows=kept_keys,
            val_rows=kept_vals,
            key_first=key_first,
            length=length,
            score_scale=score_scale,
        )
        moving_grads, grad_query = lax.scan(
            back_fn, moving_grads, (query_tiles, pos_tiles, cot_tiles, log_sum, row_dot, grad_query)
        )
        moving_grads = (
            from_behind_2(moving_grads[0].astype(jnp.bfloat16), "blk", 1).astype(jnp.float32),
            from_behind_2(moving_grads[1].astype(jnp.bfloat16), "blk", 1).astype(jnp.float32),
        )
    grad_keys, grad_vals = moving_grads
    grad_query_low = grad_query.reshape(head_shape).astype(jnp.bfloat16).astype(jnp.float32)
    grad_keys_low = grad_keys.astype(jnp.bfloat16).astype(jnp.float32)
    grad_query_pre = (
        rotate(grad_query_low, cosine, -sine_tab)
        .astype(jnp.bfloat16)
        .reshape(block_len, local_width)
    )
    grad_key_pre = (
        rotate(grad_keys_low, cosine, -sine_tab)
        .astype(jnp.bfloat16)
        .reshape(block_len, local_width)
    )
    grad_value_low = grad_vals.astype(jnp.bfloat16).reshape(block_len, local_width)
    grad_hidden_attn = lax.psum_scatter(
        (
            over_cols(grad_query_pre, full_query)
            + over_cols(grad_key_pre, full_key)
            + over_cols(grad_value_low, full_value)
        ).astype(jnp.bfloat16),
        "seq",
        scatter_dimension=0,
        tiled=True,
    ).astype(jnp.float32)
    grad_in_part, gain_attn_term = norm_back(
        input_rows_packed, inverse_attn, gain_attn_f, grad_hidden_attn
    )
    grad_wgate, grad_wup, grad_wdown = sum_mlp(grad_gate_term, grad_up_term, grad_down_term)
    grad_wquery, grad_wkey, grad_wvalue, grad_woutput, gain_attn_part, gain_mlp_part = (
        lax.psum_scatter(
            over_rows(hidden_block, grad_query_pre).astype(jnp.bfloat16),
            ("slot", "blk"),
            scatter_dimension=0,
            tiled=True,
        ).astype(jnp.float32),
        lax.psum_scatter(
            over_rows(hidden_block, grad_key_pre).astype(jnp.bfloat16),
            ("slot", "blk"),
            scatter_dimension=0,
            tiled=True,
        ).astype(jnp.float32),
        lax.psum_scatter(
            over_rows(hidden_block, grad_value_low).astype(jnp.bfloat16),
            ("slot", "blk"),
            scatter_dimension=0,
            tiled=True,
        ).astype(jnp.float32),
        lax.psum_scatter(
            grad_wout_term.astype(jnp.bfloat16), ("slot", "blk"), scatter_dimension=0, tiled=True
        ).astype(jnp.float32),
        lax.psum_scatter(
            gain_attn_term.astype(jnp.bfloat16), ("slot", "blk"), scatter_dimension=0, tiled=True
        ).astype(jnp.float32),
        lax.psum_scatter(
            gain_mlp_term.astype(jnp.bfloat16), ("slot", "blk"), scatter_dimension=0, tiled=True
        ).astype(jnp.float32),
    )
    grad_gattn, grad_gmlp = lax.psum((gain_attn_part, gain_mlp_part), "seq")
    grad_inputs = grad_resid + grad_in_part
    return (
        block_out.astype(jnp.bfloat16)[None],
        grad_inputs[None],
        grad_gattn,
        grad_wquery,
        grad_wkey,
        grad_wvalue,
        grad_woutput,
        grad_gmlp,
        grad_wgate,
        grad_wup,
        grad_wdown,
    )


def solution(mesh):
    placed = (
        P("slot", ("blk", "seq"), None),
        P("slot", ("blk", "seq"), None),
        P("slot"),
        P(("slot", "blk")),
        P(("slot", "blk"), "seq"),
        P(("slot", "blk"), "seq"),
        P(("slot", "blk"), "seq"),
        P(("slot", "blk"), "seq"),
        P(("slot", "blk")),
        P(("slot", "blk"), "seq"),
        P(("slot", "blk"), "seq"),
        P(("slot", "blk"), "seq"),
    )
    return jax.shard_map(
        shards,
        mesh=mesh,
        in_specs=placed,
        out_specs=(
            P("slot", ("blk", "seq"), None),
            P("slot", ("blk", "seq"), None),
            P(("slot", "blk")),
            P(("slot", "blk"), "seq"),
            P(("slot", "blk"), "seq"),
            P(("slot", "blk"), "seq"),
            P(("slot", "blk"), "seq"),
            P(("slot", "blk")),
            P(("slot", "blk"), "seq"),
            P(("slot", "blk"), "seq"),
            P(("slot", "blk"), "seq"),
        ),
        check_vma=False,
    )
```

profile of v0, /device:TPU:0, one launch (start us, length us, event | category | flops | bytes accessed | tf_op | source)
XLA Modules:
  0.0 2703.3 jit_solution(6175386488568458087)
XLA Ops:
  8.5 42.4 %all-gather = bf16[16,1,128]{2,1,0:T(2,128)(2,1)S(1)} all-gather(bf16[1,1,128]{2,1,0:T(2,128)(2,1)} %bitcast.279), channel_id=1, replica_groups=mesh['slot'=4,'seq'=2,'blk'=4] {'slot','blk'}, dimensions={0}, use_global_device_ids=true | all-gather | bytes 4352 | tf_op jit(solution)/shard_map/all_gather | solution.py:185
  58.4 79.9 %all-gather.18.cloned.1.call-done = bf16[2048,1024]{1,0:T(8,128)(2,1)} async-done(((bf16[128,1024]{1,0:T(8,128)(2,1)}), bf16[2048,1024]{1,0:T(8,128)(2,1)}) %all-gather.18.cloned.1.call-update) | async-done | bytes 4194320 | tf_op jit(solution)/shard_map/all_gather | solution.py:188
  142.5 73.0 %all-gather.16.cloned.1.call-done = bf16[2048,1024]{1,0:T(8,128)(2,1)} async-done(((bf16[128,1024]{1,0:T(8,128)(2,1)}), bf16[2048,1024]{1,0:T(8,128)(2,1)}) %all-gather.16.cloned.1.call-update) | async-done | bytes 4194320 | tf_op jit(solution)/shard_map/all_gather | solution.py:187
  223.3 71.0 %all-gather.20.cloned.1.call-done = bf16[2048,1024]{1,0:T(8,128)(2,1)} async-done(((bf16[128,1024]{1,0:T(8,128)(2,1)}), bf16[2048,1024]{1,0:T(8,128)(2,1)}) %all-gather.20.cloned.1.call-update) | async-done | bytes 4194320 | tf_op jit(solution)/shard_map/all_gather | solution.py:189
  307.3 14.4 collective-permute-done.1
  326.9 15.0 collective-permute-done.2
  364.6 16.0 collective-permute-done.4
  405.8 40.4 %all-gather.1 = bf16[16,1,128]{2,1,0:T(2,128)(2,1)S(1)} all-gather(bf16[1,1,128]{2,1,0:T(2,128)(2,1)S(1)} %bitcast.280), channel_id=1, replica_groups=mesh['slot'=4,'seq'=2,'blk'=4] {'slot','blk'}, dimensions={0}, use_global_device_ids=true | all-gather | bytes 4352 | tf_op jit(solution)/shard_map/all_gather | solution.py:186
  456.0 195.9 %all-gather.28.cloned.1.call-done = bf16[2048,4096]{1,0:T(8,128)(2,1)} async-done(((bf16[128,4096]{1,0:T(8,128)(2,1)}), bf16[2048,4096]{1,0:T(8,128)(2,1)}) %all-gather.28.cloned.1.call-update) | async-done | bytes 16777232 | tf_op jit(solution)/shard_map/all_gather | solution.py:192
  652.0 12.6 fusion.191
  664.6 180.3 %all-gather.26.cloned.1.call-done = bf16[2048,4096]{1,0:T(8,128)(2,1)} async-done(((bf16[128,4096]{1,0:T(8,128)(2,1)}), bf16[2048,4096]{1,0:T(8,128)(2,1)}) %all-gather.26.cloned.1.call-update) | async-done | bytes 16777232 | tf_op jit(solution)/shard_map/all_gather | solution.py:191
  855.1 195.1 %all-gather.30.cloned.1.call-done = bf16[2048,4096]{1,0:T(8,128)(2,1)} async-done(((bf16[128,4096]{1,0:T(8,128)(2,1)}), bf16[2048,4096]{1,0:T(8,128)(2,1)}) %all-gather.30.cloned.1.call-update) | async-done | bytes 16777232 | tf_op jit(solution)/shard_map/all_gather | solution.py:193
  1050.2 13.4 multiply_convert_fusion.4
  1063.6 12.3 fusion.192
  1075.9 12.5 fusion.12
  1180.1 11.0 collective-permute-done.8
  1227.4 12.3 convolution_convert_fusion.7
  1292.5 44.2 %all-reduce.3 = (bf16[2048]{0:T(1024)(128)(2,1)S(1)}, bf16[2048]{0:T(1024)(128)(2,1)S(1)}) all-reduce(bf16[2048]{0:T(1024)(128)(2,1)S(1)} %get-tuple-element.228, bf16[2048]{0:T(1024)(128)(2,1)S(1)} %copy-done.53), channel_id=6, replica_groups=mesh['slot'=4,'seq'=2,'blk'=4] {'slot','blk'}, use_global_device_ids=true, to_apply=%region_18.19.clone | all-reduce | flops 4096 | bytes 16384
  1351.5 95.0 %reduce-scatter.24.cloned.1.call-done = bf16[128,1024]{1,0:T(8,128)(2,1)} async-done(((bf16[2048,1024]{1,0:T(8,128)(2,1)}), bf16[128,1024]{1,0:T(8,128)(2,1)}) %reduce-scatter.24.cloned.1.call-update) | async-done | bytes 262160 | tf_op jit(solution)/shard_map/reduce_scatter | solution.py:341
  1448.3 95.0 %reduce-scatter.22.cloned.1.call-done = bf16[128,1024]{1,0:T(8,128)(2,1)} async-done(((bf16[2048,1024]{1,0:T(8,128)(2,1)}), bf16[128,1024]{1,0:T(8,128)(2,1)}) %reduce-scatter.22.cloned.1.call-update) | async-done | bytes 262160 | tf_op jit(solution)/shard_map/reduce_scatter | solution.py:335
  1545.2 95.2 %reduce-scatter.20.cloned.1.call-done = bf16[128,1024]{1,0:T(8,128)(2,1)} async-done(((bf16[2048,1024]{1,0:T(8,128)(2,1)}), bf16[128,1024]{1,0:T(8,128)(2,1)}) %reduce-scatter.20.cloned.1.call-update) | async-done | bytes 262160 | tf_op jit(solution)/shard_map/reduce_scatter | solution.py:329
  1642.1 348.7 %reduce-scatter.30.cloned.1.call-done = bf16[128,4096]{1,0:T(8,128)(2,1)} async-done(((bf16[2048,4096]{1,0:T(8,128)(2,1)}), bf16[128,4096]{1,0:T(8,128)(2,1)}) %reduce-scatter.30.cloned.1.call-update) | async-done | bytes 1048592 | tf_op jit(solution)/shard_map/reduce_scatter | solution.py:131
  1993.6 348.6 %reduce-scatter.28.cloned.1.call-done = bf16[128,4096]{1,0:T(8,128)(2,1)} async-done(((bf16[2048,4096]{1,0:T(8,128)(2,1)}), bf16[128,4096]{1,0:T(8,128)(2,1)}) %reduce-scatter.28.cloned.1.call-update) | async-done | bytes 1048592 | tf_op jit(solution)/shard_map/reduce_scatter | solution.py:128
  2344.9 348.6 %reduce-scatter.32.cloned.1.call-done = bf16[128,4096]{1,0:T(8,128)(2,1)} async-done(((bf16[2048,4096]{1,0:T(8,128)(2,1)}), bf16[128,4096]{1,0:T(8,128)(2,1)}) %reduce-scatter.32.cloned.1.call-update) | async-done | bytes 1048592 | tf_op jit(solution)/shard_map/reduce_scatter | solution.py:134
  (312 shorter events, 313.4 us)
Async XLA Ops:
  7.2 51.2 %all-gather.14.cloned.1.call-start = ((), (), s32[]{:S(2)}) async-start(), calls=%async_computation.11 | async-start | bytes 1572864 | tf_op jit(solution)/shard_map/all_gather | solution.py:199
  52.9 85.3 %all-gather.18.cloned.1.call-start = ((), (), s32[]{:S(2)}) async-start(), calls=%async_computation.13 | async-start | bytes 4456448 | tf_op jit(solution)/shard_map/all_gather | solution.py:188
  53.7 161.9 %all-gather.16.cloned.1.call-start = ((), (), s32[]{:S(2)}) async-start(), calls=%async_computation.12 | async-start | bytes 4456448 | tf_op jit(solution)/shard_map/all_gather | solution.py:187
  54.4 239.9 %all-gather.20.cloned.1.call-start = ((), (), s32[]{:S(2)}) async-start(), calls=%async_computation.14 | async-start | bytes 4456448 | tf_op jit(solution)/shard_map/all_gather | solution.py:189
  55.0 345.5 %all-gather.22.cloned.1.call-start = ((), (), s32[]{:S(2)}) async-start(), calls=%async_computation.15 | async-start | bytes 4456448 | tf_op jit(solution)/shard_map/all_gather | solution.py:190
  55.6 390.7 %reduce-scatter.12.cloned.1.call-start = ((), (), s32[]{:S(2)}) async-start(), calls=%async_computation.16 | async-start | bytes 1572864 | tf_op jit(solution)/shard_map/reduce_scatter | solution.py:234
  219.9 84.1 %collective-permute-start = (bf16[256,16,64]{0,2,1:T(8,128)(2,1)S(1)}, bf16[256,16,64]{0,2,1:T(8,128)(2,1)S(1)}, u32[]{:S(2)}, u32[]{:S(2)}) collective-permute-start(bf16[256,16,64]{0,2,1:T(8,128)(2,1)S(1)} %pad_maximum_fusion.1), channel_id=1, source_target_pairs={{0,1},{1,2},{2,3},{4,5},{5,6},{6,7},{8,9},{9,10},{10,11},{12,13},{... | collective-permute-start | bytes 1572872 | tf_op jit(solution)/shard_map/ppermute | solution.py:16
  341.9 38.7 %collective-permute-start.4 = (bf16[256,16,64]{0,2,1:T(8,128)(2,1)S(1)}, bf16[256,16,64]{0,2,1:T(8,128)(2,1)S(1)}, u32[]{:S(2)}, u32[]{:S(2)}) collective-permute-start(bf16[256,16,64]{0,2,1:T(8,128)(2,1)S(1)} %collective-permute-done.2), channel_id=1, source_target_pairs={{0,1},{1,2},{2,3},{4,5},{5,6},{6,7},{8,9},{9,10},{10,11},{12,13},{... | collective-permute-start | bytes 1572872 | tf_op jit(solution)/shard_map/ppermute | solution.py:16
  358.2 40.3 %collective-permute-start.5 = (bf16[256,16,64]{0,2,1:T(8,128)(2,1)S(1)}, bf16[256,16,64]{0,2,1:T(8,128)(2,1)S(1)}, u32[]{:S(2)}, u32[]{:S(2)}) collective-permute-start(bf16[256,16,64]{0,2,1:T(8,128)(2,1)S(1)} %collective-permute-done.3), channel_id=1, source_target_pairs={{0,1},{1,2},{2,3},{4,5},{5,6},{6,7},{8,9},{9,10},{10,11},{12,13},{... | collective-permute-start | bytes 1572872 | tf_op jit(solution)/shard_map/ppermute | solution.py:16
  405.7 50.3 %all-gather.24.cloned.1.call-start = ((), (), s32[]{:S(2)}) async-start(), calls=%async_computation.17 | async-start | bytes 1572864 | tf_op jit(solution)/shard_map/all_gather | solution.py:242
  449.6 202.3 %all-gather.28.cloned.1.call-start = ((), (), s32[]{:S(2)}) async-start(), calls=%async_computation.19 | async-start | bytes 17825792 | tf_op jit(solution)/shard_map/all_gather | solution.py:192
  450.4 394.6 %all-gather.26.cloned.1.call-start = ((), (), s32[]{:S(2)}) async-start(), calls=%async_computation.18 | async-start | bytes 17825792 | tf_op jit(solution)/shard_map/all_gather | solution.py:191
  451.1 404.0 %all-gather.32.cloned.1.call-start = ((), (), s32[]{:S(2)}) async-start(), calls=%async_computation.22 | async-start | bytes 1572864 | tf_op jit(solution)/shard_map/all_gather | solution.py:255
  452.2 598.0 %all-gather.30.cloned.1.call-start = ((), (), s32[]{:S(2)}) async-start(), calls=%async_computation.20 | async-start | bytes 17825792 | tf_op jit(solution)/shard_map/all_gather | solution.py:193
  452.9 642.4 %reduce-scatter.16.cloned.1.call-start = ((), (), s32[]{:S(2)}) async-start(), calls=%async_computation.23 | async-start | bytes 1572864 | tf_op jit(solution)/shard_map/reduce_scatter | solution.py:264
  1100.3 190.6 %reduce-scatter.18.cloned.1.call-start = ((), (), s32[]{:S(2)}) async-start(), calls=%async_computation.25 | async-start | bytes 1572864 | tf_op jit(solution)/shard_map/reduce_scatter | solution.py:314
  1227.4 112.4 %reduce-scatter.14.cloned.1.call-start = ((), (), s32[]{:S(2)}) async-start(), calls=%async_computation.21 | async-start | bytes 1572864 | tf_op jit(solution)/shard_map/reduce_scatter | solution.py:247
  1239.7 110.0 %reduce-scatter.26.cloned.1.call-start = ((), (), s32[]{:S(2)}) async-start(), calls=%async_computation.29 | async-start | bytes 4456448 | tf_op jit(solution)/shard_map/reduce_scatter | solution.py:347
  1244.7 201.8 %reduce-scatter.24.cloned.1.call-start = ((), (), s32[]{:S(2)}) async-start(), calls=%async_computation.28 | async-start | bytes 4456448 | tf_op jit(solution)/shard_map/reduce_scatter | solution.py:341
  1249.1 294.2 %reduce-scatter.22.cloned.1.call-start = ((), (), s32[]{:S(2)}) async-start(), calls=%async_computation.27 | async-start | bytes 4456448 | tf_op jit(solution)/shard_map/reduce_scatter | solution.py:335
  1252.6 387.7 %reduce-scatter.20.cloned.1.call-start = ((), (), s32[]{:S(2)}) async-start(), calls=%async_computation.26 | async-start | bytes 4456448 | tf_op jit(solution)/shard_map/reduce_scatter | solution.py:329
  1256.9 733.9 %reduce-scatter.30.cloned.1.call-start = ((), (), s32[]{:S(2)}) async-start(), calls=%async_computation.31 | async-start | bytes 17825792 | tf_op jit(solution)/shard_map/reduce_scatter | solution.py:131
  1268.0 1074.2 %reduce-scatter.28.cloned.1.call-start = ((), (), s32[]{:S(2)}) async-start(), calls=%async_computation.30 | async-start | bytes 17825792 | tf_op jit(solution)/shard_map/reduce_scatter | solution.py:128
  1277.9 1415.5 %reduce-scatter.32.cloned.1.call-start = ((), (), s32[]{:S(2)}) async-start(), calls=%async_computation.32 | async-start | bytes 17825792 | tf_op jit(solution)/shard_map/reduce_scatter | solution.py:134
  (81 other events, 2319.7 us)
Sparse Core Ops, SparseCore 0:
  53.0 5.3 all-gather.13
  61.1 77.0 all-gather.17
  141.0 74.4 all-gather.15
  218.1 76.0 all-gather.19
  296.9 100.4 all-gather.21
  405.9 9.3 reduce-scatter.11
  449.8 6.2 all-gather.23
  459.2 192.7 all-gather.27
  655.1 189.7 all-gather.25
  847.0 7.2 all-gather.31
  857.4 192.7 all-gather.29
  1088.6 6.7 reduce-scatter.15
  1100.4 10.1 all-gather.33
  1227.5 7.8 reduce-scatter.17
  1239.8 7.5 reduce-scatter.13
  1249.5 100.1 reduce-scatter.25
  1351.9 94.6 reduce-scatter.23
  1448.7 94.6 reduce-scatter.21
  1545.7 94.6 reduce-scatter.19
  1642.5 348.3 reduce-scatter.29
  1993.1 348.9 reduce-scatter.27
  2344.4 348.9 reduce-scatter.31
where the time goes:
time: 2710 us; the launch traced here: 2700 us
  waiting for transfers between devices  2300 us (85%)
  matrix products  172 us (6%)
  blocking collectives  130 us (5%)
  other arithmetic  41.5 us (2%)
  starting transfers between devices  30.1 us (1%)
    reduce_scatter x1, waiting for transfers between devices, sum_mlp(): lax.psum_scatter(term_up.astype(jnp.bfloat16), ('slot', 'blk'), scatter_d...  349 us
    reduce_scatter x1, waiting for transfers between devices, sum_mlp(): lax.psum_scatter(term_down.astype(jnp.bfloat16), ('slot', 'blk'), scatter...  349 us
    reduce_scatter x1, waiting for transfers between devices, sum_mlp(): lax.psum_scatter(term_gate.astype(jnp.bfloat16), ('slot', 'blk'), scatter...  349 us
    all_gather x1, waiting for transfers between devices, shards(): lax.all_gather(up_weight, ('slot', 'blk'), axis=0, tiled=True)  196 us
    all_gather x1, waiting for transfers between devices, shards(): lax.all_gather(down_weight, ('slot', 'blk'), axis=0, tiled=True)  195 us
    all_gather x1, waiting for transfers between devices, shards(): lax.all_gather(gate_weight, ('slot', 'blk'), axis=0, tiled=True)  180 us
    reduce_scatter x1, waiting for transfers between devices, shards(): lax.psum_scatter(over_rows(hidden_block, grad_query_pre).astype(jnp.bfloa...  95.2 us
    reduce_scatter x1, waiting for transfers between devices, shards(): lax.psum_scatter(over_rows(hidden_block, grad_key_pre).astype(jnp.bfloat1...  95 us
  transfers between devices with their start and end apart: 36, of which 30 were waited for; matrix products, arithmetic and copies ran while one was open for 5% of the time, Pallas kernels for 0%

commit v1 on v0

--- a/solution.py
+++ b/solution.py
@@ -3,6 +3,7 @@
 import jax.numpy as jnp
 from jax import lax
 from jax.sharding import PartitionSpec as P
+from jax.lax import axis_index, axis_size, ppermute
 
 HEADS = 32
 HEAD_DIM = 64
@@ -171,6 +172,24 @@
     tile_count = block_len // tile_rows
     tiled_shape = (tile_count, tile_rows, local_heads, HEAD_DIM)
     pos_tiles = block_pos.reshape(tile_count, tile_rows)
+
+    def skins_mark(my_data):
+        f_next = axis_size(("slot", "blk"))
+        later = axis_index(("slot", "blk"))
+        item_now, r1, n_now = (f_next, later, my_data.shape[0])
+        pieces_in = [t * item_now if dev_i == 0 else t for dev_i, t in enumerate(my_data.shape)]
+        k_now = jnp.zeros(pieces_in, my_data.dtype)
+        low = lax.dynamic_update_slice_in_dim(k_now, my_data, r1 * n_now, axis=0)
+        for rr in range(1, item_now):
+            p_next = range(item_now)
+            u1 = map(lambda dev_i: (dev_i, (dev_i + 1) % item_now), p_next)
+            work_now = list(u1)
+            my_data = ppermute(my_data, ("slot", "blk"), work_now)
+            low = lax.dynamic_update_slice_in_dim(
+                low, my_data, (r1 - rr) % item_now * n_now, axis=0
+            )
+        return low
+
     (
         gain_attn,
         gain_mlp,
@@ -188,7 +207,7 @@
         lax.all_gather(w_key, ("slot", "blk"), axis=0, tiled=True),
         lax.all_gather(w_value, ("slot", "blk"), axis=0, tiled=True),
         lax.all_gather(output_weight, ("slot", "blk"), axis=0, tiled=True),
-        lax.all_gather(gate_weight, ("slot", "blk"), axis=0, tiled=True),
+        skins_mark(gate_weight),
         lax.all_gather(up_weight, ("slot", "blk"), axis=0, tiled=True),
         lax.all_gather(down_weight, ("slot", "blk"), axis=0, tiled=True),
     )

time: 2710 us -> 2810 us (1.037)
  waiting for transfers between devices: 2300 us -> 2340 us
  local copies, waits for them, and re-layouts: 14.2 us -> 48.9 us
    ppermute x0 -> x15, waiting for transfers between devices: none -> 613 us  [skins_mark(): my_data = ppermute(my_data, ('slot', 'blk'), work_now)]
    all_gather x1, waiting for transfers between devices: 196 us -> 0.01 us  [shards(): lax.all_gather(up_weight, ('slot', 'blk'), axis=0, tiled=True)]
    all_gather x1, waiting for transfers between devices: 195 us -> 0.01 us  [shards(): lax.all_gather(down_weight, ('slot', 'blk'), axis=0, tiled=True)]
    all_gather x1 -> x0, waiting for transfers between devices: 180 us -> none  [shards(): lax.all_gather(gate_weight, ('slot', 'blk'), axis=0, tiled=True)]
  transfers between devices with their start and end apart: 36 -> 50, of which waited for: 30 -> 40; matrix products, arithmetic and copies ran while one was open for 5% -> 6% of each run, Pallas kernels for 0% -> 0%
where the time goes in v1:
time: 2810 us; the launch traced here: 2800 us
  waiting for transfers between devices  2340 us (83%)
  matrix products  169 us (6%)
  blocking collectives  128 us (5%)
  starting transfers between devices  54.4 us (2%)
  local copies, waits for them, and re-layouts  48.9 us (2%)
  other arithmetic  40.2 us (1%)
    ppermute x15, waiting for transfers between devices, skins_mark(): my_data = ppermute(my_data, ('slot', 'blk'), work_now)  613 us
    reduce_scatter x1, waiting for transfers between devices, sum_mlp(): lax.psum_scatter(term_gate.astype(jnp.bfloat16), ('slot', 'blk'), scatter...  349 us
    reduce_scatter x1, waiting for transfers between devices, sum_mlp(): lax.psum_scatter(term_down.astype(jnp.bfloat16), ('slot', 'blk'), scatter...  349 us
    reduce_scatter x1, waiting for transfers between devices, sum_mlp(): lax.psum_scatter(term_up.astype(jnp.bfloat16), ('slot', 'blk'), scatter_d...  348 us
    reduce_scatter x1, waiting for transfers between devices, shards(): lax.psum_scatter(over_rows(hidden_block, grad_value_low).astype(jnp.bfloa...  95 us
    reduce_scatter x1, waiting for transfers between devices, shards(): lax.psum_scatter(over_rows(hidden_block, grad_query_pre).astype(jnp.bfloa...  95 us
    reduce_scatter x1, waiting for transfers between devices, shards(): lax.psum_scatter(over_rows(hidden_block, grad_key_pre).astype(jnp.bfloat1...  95 us
    all_gather x1, waiting for transfers between devices, shards(): lax.all_gather(w_query, ('slot', 'blk'), axis=0, tiled=True)  79.9 us
  transfers between devices with their start and end apart: 50, of which 40 were waited for; matrix products, arithmetic and copies ran while one was open for 6% of the time, Pallas kernels for 0%

profile of v1, /device:TPU:0, one launch (start us, length us, event | category | flops | bytes accessed | tf_op | source)
XLA Modules:
  0.0 2801.2 jit_solution(16790176681354446307)
XLA Ops:
  7.2 42.4 %all-gather = bf16[16,1,128]{2,1,0:T(2,128)(2,1)S(1)} all-gather(bf16[1,1,128]{2,1,0:T(2,128)(2,1)} %bitcast.279), channel_id=1, replica_groups=mesh['slot'=4,'seq'=2,'blk'=4] {'slot','blk'}, dimensions={0}, use_global_device_ids=true | all-gather | bytes 4352 | tf_op jit(solution)/shard_map/all_gather | solution.py:204
  58.4 79.9 %all-gather.15.cloned.1.call-done = bf16[2048,1024]{1,0:T(8,128)(2,1)} async-done(((bf16[128,1024]{1,0:T(8,128)(2,1)}), bf16[2048,1024]{1,0:T(8,128)(2,1)}) %all-gather.15.cloned.1.call-update) | async-done | bytes 4194320 | tf_op jit(solution)/shard_map/all_gather | solution.py:206
  142.5 73.0 %all-gather.17.cloned.1.call-done = bf16[2048,1024]{1,0:T(8,128)(2,1)} async-done(((bf16[128,1024]{1,0:T(8,128)(2,1)}), bf16[2048,1024]{1,0:T(8,128)(2,1)}) %all-gather.17.cloned.1.call-update) | async-done | bytes 4194320 | tf_op jit(solution)/shard_map/all_gather | solution.py:207
  223.3 71.0 %all-gather.19.cloned.1.call-done = bf16[2048,1024]{1,0:T(8,128)(2,1)} async-done(((bf16[128,1024]{1,0:T(8,128)(2,1)}), bf16[2048,1024]{1,0:T(8,128)(2,1)}) %all-gather.19.cloned.1.call-update) | async-done | bytes 4194320 | tf_op jit(solution)/shard_map/all_gather | solution.py:208
  405.8 40.4 %all-gather.1 = bf16[16,1,128]{2,1,0:T(2,128)(2,1)S(1)} all-gather(bf16[1,1,128]{2,1,0:T(2,128)(2,1)S(1)} %bitcast.280), channel_id=1, replica_groups=mesh['slot'=4,'seq'=2,'blk'=4] {'slot','blk'}, dimensions={0}, use_global_device_ids=true | all-gather | bytes 4352 | tf_op jit(solution)/shard_map/all_gather | solution.py:205
  475.9 45.5 %collective-permute-done.7 = bf16[128,4096]{1,0:T(8,128)(2,1)S(1)} collective-permute-done((bf16[128,4096]{1,0:T(8,128)(2,1)S(1)}, bf16[128,4096]{1,0:T(8,128)(2,1)S(1)}, u32[]{:S(2)}, u32[]{:S(2)}) %collective-permute-start.7) | collective-permute-done | bytes 1048608 | tf_op jit(solution)/shard_map/ppermute | solution.py:187
  522.4 49.0 %collective-permute-done.8 = bf16[128,4096]{1,0:T(8,128)(2,1)S(1)} collective-permute-done((bf16[128,4096]{1,0:T(8,128)(2,1)S(1)}, bf16[128,4096]{1,0:T(8,128)(2,1)S(1)}, u32[]{:S(2)}, u32[]{:S(2)}) %collective-permute-start.8) | collective-permute-done | bytes 1048608 | tf_op jit(solution)/shard_map/ppermute | solution.py:187
  574.4 42.5 %collective-permute-done.9 = bf16[128,4096]{1,0:T(8,128)(2,1)S(1)} collective-permute-done((bf16[128,4096]{1,0:T(8,128)(2,1)S(1)}, bf16[128,4096]{1,0:T(8,128)(2,1)S(1)}, u32[]{:S(2)}, u32[]{:S(2)}) %collective-permute-start.9) | collective-permute-done | bytes 1048608 | tf_op jit(solution)/shard_map/ppermute | solution.py:187
  617.0 51.1 %collective-permute-done.10 = bf16[128,4096]{1,0:T(8,128)(2,1)S(1)} collective-permute-done((bf16[128,4096]{1,0:T(8,128)(2,1)S(1)}, bf16[128,4096]{1,0:T(8,128)(2,1)S(1)}, u32[]{:S(2)}, u32[]{:S(2)}) %collective-permute-start.10) | collective-permute-done | bytes 1048608 | tf_op jit(solution)/shard_map/ppermute | solution.py:187
  671.2 60.8 %collective-permute-done.11 = bf16[128,4096]{1,0:T(8,128)(2,1)S(1)} collective-permute-done((bf16[128,4096]{1,0:T(8,128)(2,1)S(1)}, bf16[128,4096]{1,0:T(8,128)(2,1)S(1)}, u32[]{:S(2)}, u32[]{:S(2)}) %collective-permute-start.11) | collective-permute-done | bytes 1048608 | tf_op jit(solution)/shard_map/ppermute | solution.py:187
  741.5 35.0 %collective-permute-done.12 = bf16[128,4096]{1,0:T(8,128)(2,1)S(1)} collective-permute-done((bf16[128,4096]{1,0:T(8,128)(2,1)S(1)}, bf16[128,4096]{1,0:T(8,128)(2,1)S(1)}, u32[]{:S(2)}, u32[]{:S(2)}) %collective-permute-start.12) | collective-permute-done | bytes 1048608 | tf_op jit(solution)/shard_map/ppermute | solution.py:187
  777.6 50.1 %collective-permute-done.13 = bf16[128,4096]{1,0:T(8,128)(2,1)S(1)} collective-permute-done((bf16[128,4096]{1,0:T(8,128)(2,1)S(1)}, bf16[128,4096]{1,0:T(8,128)(2,1)S(1)}, u32[]{:S(2)}, u32[]{:S(2)}) %collective-permute-start.13) | collective-permute-done | bytes 1048608 | tf_op jit(solution)/shard_map/ppermute | solution.py:187
  828.7 50.0 %collective-permute-done.14 = bf16[128,4096]{1,0:T(8,128)(2,1)} collective-permute-done((bf16[128,4096]{1,0:T(8,128)(2,1)S(1)}, bf16[128,4096]{1,0:T(8,128)(2,1)}, u32[]{:S(2)}, u32[]{:S(2)}) %collective-permute-start.14) | collective-permute-done | bytes 1048608 | tf_op jit(solution)/shard_map/ppermute | solution.py:187
  878.7 45.2 %collective-permute-done.15 = bf16[128,4096]{1,0:T(8,128)(2,1)} collective-permute-done((bf16[128,4096]{1,0:T(8,128)(2,1)}, bf16[128,4096]{1,0:T(8,128)(2,1)}, u32[]{:S(2)}, u32[]{:S(2)}) %collective-permute-start.15) | collective-permute-done | bytes 1048608 | tf_op jit(solution)/shard_map/ppermute | solution.py:187
  935.9 38.2 %collective-permute-done.16 = bf16[128,4096]{1,0:T(8,128)(2,1)} collective-permute-done((bf16[128,4096]{1,0:T(8,128)(2,1)}, bf16[128,4096]{1,0:T(8,128)(2,1)}, u32[]{:S(2)}, u32[]{:S(2)}) %collective-permute-start.16) | collective-permute-done | bytes 1048608 | tf_op jit(solution)/shard_map/ppermute | solution.py:187
  977.3 53.7 %collective-permute-done.17 = bf16[128,4096]{1,0:T(8,128)(2,1)S(1)} collective-permute-done((bf16[128,4096]{1,0:T(8,128)(2,1)}, bf16[128,4096]{1,0:T(8,128)(2,1)S(1)}, u32[]{:S(2)}, u32[]{:S(2)}) %collective-permute-start.17) | collective-permute-done | bytes 1048608 | tf_op jit(solution)/shard_map/ppermute | solution.py:187
  1039.5 43.2 %collective-permute-done.18 = bf16[128,4096]{1,0:T(8,128)(2,1)S(1)} collective-permute-done((bf16[128,4096]{1,0:T(8,128)(2,1)S(1)}, bf16[128,4096]{1,0:T(8,128)(2,1)S(1)}, u32[]{:S(2)}, u32[]{:S(2)}) %collective-permute-start.18) | collective-permute-done | bytes 1048608 | tf_op jit(solution)/shard_map/ppermute | solution.py:187
  1391.0 42.1 %all-reduce.3 = (bf16[2048]{0:T(1024)(128)(2,1)S(1)}, bf16[2048]{0:T(1024)(128)(2,1)S(1)}) all-reduce(bf16[2048]{0:T(1024)(128)(2,1)S(1)} %get-tuple-element.228, bf16[2048]{0:T(1024)(128)(2,1)S(1)} %copy-done.67), channel_id=6, replica_groups=mesh['slot'=4,'seq'=2,'blk'=4] {'slot','blk'}, use_global_device_ids=true, to_apply=%region_18.19.clone | all-reduce | flops 4096 | bytes 16384
  1449.5 95.0 %reduce-scatter.24.cloned.1.call-done = bf16[128,1024]{1,0:T(8,128)(2,1)} async-done(((bf16[2048,1024]{1,0:T(8,128)(2,1)}), bf16[128,1024]{1,0:T(8,128)(2,1)}) %reduce-scatter.24.cloned.1.call-update) | async-done | bytes 262160 | tf_op jit(solution)/shard_map/reduce_scatter | solution.py:360
  1546.3 95.0 %reduce-scatter.22.cloned.1.call-done = bf16[128,1024]{1,0:T(8,128)(2,1)} async-done(((bf16[2048,1024]{1,0:T(8,128)(2,1)}), bf16[128,1024]{1,0:T(8,128)(2,1)}) %reduce-scatter.22.cloned.1.call-update) | async-done | bytes 262160 | tf_op jit(solution)/shard_map/reduce_scatter | solution.py:354
  1643.2 95.0 %reduce-scatter.20.cloned.1.call-done = bf16[128,1024]{1,0:T(8,128)(2,1)} async-done(((bf16[2048,1024]{1,0:T(8,128)(2,1)}), bf16[128,1024]{1,0:T(8,128)(2,1)}) %reduce-scatter.20.cloned.1.call-update) | async-done | bytes 262160 | tf_op jit(solution)/shard_map/reduce_scatter | solution.py:348
  1740.0 348.9 %reduce-scatter.28.cloned.1.call-done = bf16[128,4096]{1,0:T(8,128)(2,1)} async-done(((bf16[2048,4096]{1,0:T(8,128)(2,1)}), bf16[128,4096]{1,0:T(8,128)(2,1)}) %reduce-scatter.28.cloned.1.call-update) | async-done | bytes 1048592 | tf_op jit(solution)/shard_map/reduce_scatter | solution.py:129
  2091.6 348.4 %reduce-scatter.30.cloned.1.call-done = bf16[128,4096]{1,0:T(8,128)(2,1)} async-done(((bf16[2048,4096]{1,0:T(8,128)(2,1)}), bf16[128,4096]{1,0:T(8,128)(2,1)}) %reduce-scatter.30.cloned.1.call-update) | async-done | bytes 1048592 | tf_op jit(solution)/shard_map/reduce_scatter | solution.py:132
  2442.8 348.5 %reduce-scatter.32.cloned.1.call-done = bf16[128,4096]{1,0:T(8,128)(2,1)} async-done(((bf16[2048,4096]{1,0:T(8,128)(2,1)}), bf16[128,4096]{1,0:T(8,128)(2,1)}) %reduce-scatter.32.cloned.1.call-update) | async-done | bytes 1048592 | tf_op jit(solution)/shard_map/reduce_scatter | solution.py:135
  (386 shorter events, 540.2 us)
Async XLA Ops:
  7.2 51.2 %all-gather.13.cloned.1.call-start = ((), (), s32[]{:S(2)}) async-start(), calls=%async_computation.11 | async-start | bytes 1572864 | tf_op jit(solution)/shard_map/all_gather | solution.py:218
  52.9 85.3 %all-gather.15.cloned.1.call-start = ((), (), s32[]{:S(2)}) async-start(), calls=%async_computation.12 | async-start | bytes 4456448 | tf_op jit(solution)/shard_map/all_gather | solution.py:206
  53.7 161.9 %all-gather.17.cloned.1.call-start = ((), (), s32[]{:S(2)}) async-start(), calls=%async_computation.13 | async-start | bytes 4456448 | tf_op jit(solution)/shard_map/all_gather | solution.py:207
  54.4 239.9 %all-gather.19.cloned.1.call-start = ((), (), s32[]{:S(2)}) async-start(), calls=%async_computation.14 | async-start | bytes 4456448 | tf_op jit(solution)/shard_map/all_gather | solution.py:208
  55.0 345.5 %all-gather.21.cloned.1.call-start = ((), (), s32[]{:S(2)}) async-start(), calls=%async_computation.15 | async-start | bytes 4456448 | tf_op jit(solution)/shard_map/all_gather | solution.py:209
  55.6 390.7 %reduce-scatter.12.cloned.1.call-start = ((), (), s32[]{:S(2)}) async-start(), calls=%async_computation.16 | async-start | bytes 1572864 | tf_op jit(solution)/shard_map/reduce_scatter | solution.py:253
  219.9 84.1 %collective-permute-start = (bf16[256,16,64]{0,2,1:T(8,128)(2,1)S(1)}, bf16[256,16,64]{0,2,1:T(8,128)(2,1)S(1)}, u32[]{:S(2)}, u32[]{:S(2)}) collective-permute-start(bf16[256,16,64]{0,2,1:T(8,128)(2,1)S(1)} %pad_maximum_fusion.1), channel_id=1, source_target_pairs={{0,1},{1,2},{2,3},{4,5},{5,6},{6,7},{8,9},{9,10},{10,11},{12,13},{... | collective-permute-start | bytes 1572872 | tf_op jit(solution)/shard_map/ppermute | solution.py:17
  405.7 716.1 %all-gather.23.cloned.1.call-start = ((), (), s32[]{:S(2)}) async-start(), calls=%async_computation.17 | async-start | bytes 1572864 | tf_op jit(solution)/shard_map/all_gather | solution.py:261
  449.6 672.2 %all-gather.25.cloned.1.call-start = ((), (), s32[]{:S(2)}) async-start(), calls=%async_computation.18 | async-start | bytes 17825792 | tf_op jit(solution)/shard_map/all_gather | solution.py:211
  450.4 684.1 %all-gather.29.cloned.1.call-start = ((), (), s32[]{:S(2)}) async-start(), calls=%async_computation.21 | async-start | bytes 1572864 | tf_op jit(solution)/shard_map/all_gather | solution.py:274
  451.5 683.0 %all-gather.27.cloned.1.call-start = ((), (), s32[]{:S(2)}) async-start(), calls=%async_computation.19 | async-start | bytes 17825792 | tf_op jit(solution)/shard_map/all_gather | solution.py:212
  452.1 737.2 %reduce-scatter.16.cloned.1.call-start = ((), (), s32[]{:S(2)}) async-start(), calls=%async_computation.22 | async-start | bytes 1572864 | tf_op jit(solution)/shard_map/reduce_scatter | solution.py:283
  668.0 63.9 %collective-permute-start.11 = (bf16[128,4096]{1,0:T(8,128)(2,1)S(1)}, bf16[128,4096]{1,0:T(8,128)(2,1)S(1)}, u32[]{:S(2)}, u32[]{:S(2)}) collective-permute-start(bf16[128,4096]{1,0:T(8,128)(2,1)S(1)} %collective-permute-done.10), channel_id=1, source_target_pairs={{0,1},{1,2},{2,3},{3,8},{8,9},{9,10},{10,11},{11,16},{16,17},{17,1... | collective-permute-start | bytes 3145736 | tf_op jit(solution)/shard_map/ppermute | solution.py:187
  974.1 56.9 %collective-permute-start.17 = (bf16[128,4096]{1,0:T(8,128)(2,1)}, bf16[128,4096]{1,0:T(8,128)(2,1)S(1)}, u32[]{:S(2)}, u32[]{:S(2)}) collective-permute-start(bf16[128,4096]{1,0:T(8,128)(2,1)} %collective-permute-done.16), channel_id=1, source_target_pairs={{0,1},{1,2},{2,3},{3,8},{8,9},{9,10},{10,11},{11,16},{16,17},{17,1... | collective-permute-start | bytes 3145736 | tf_op jit(solution)/shard_map/ppermute | solution.py:187
  1031.0 51.8 %collective-permute-start.18 = (bf16[128,4096]{1,0:T(8,128)(2,1)S(1)}, bf16[128,4096]{1,0:T(8,128)(2,1)S(1)}, u32[]{:S(2)}, u32[]{:S(2)}) collective-permute-start(bf16[128,4096]{1,0:T(8,128)(2,1)S(1)} %collective-permute-done.17), channel_id=1, source_target_pairs={{0,1},{1,2},{2,3},{3,8},{8,9},{9,10},{10,11},{11,16},{16,17},{17,1... | collective-permute-start | bytes 3145736 | tf_op jit(solution)/shard_map/ppermute | solution.py:187
  1194.3 195.1 %reduce-scatter.18.cloned.1.call-start = ((), (), s32[]{:S(2)}) async-start(), calls=%async_computation.24 | async-start | bytes 1572864 | tf_op jit(solution)/shard_map/reduce_scatter | solution.py:333
  1326.0 110.1 %reduce-scatter.14.cloned.1.call-start = ((), (), s32[]{:S(2)}) async-start(), calls=%async_computation.20 | async-start | bytes 1572864 | tf_op jit(solution)/shard_map/reduce_scatter | solution.py:266
  1338.4 109.3 %reduce-scatter.26.cloned.1.call-start = ((), (), s32[]{:S(2)}) async-start(), calls=%async_computation.28 | async-start | bytes 4456448 | tf_op jit(solution)/shard_map/reduce_scatter | solution.py:366
  1343.3 201.2 %reduce-scatter.24.cloned.1.call-start = ((), (), s32[]{:S(2)}) async-start(), calls=%async_computation.27 | async-start | bytes 4456448 | tf_op jit(solution)/shard_map/reduce_scatter | solution.py:360
  1347.8 293.6 %reduce-scatter.22.cloned.1.call-start = ((), (), s32[]{:S(2)}) async-start(), calls=%async_computation.26 | async-start | bytes 4456448 | tf_op jit(solution)/shard_map/reduce_scatter | solution.py:354
  1351.2 386.9 %reduce-scatter.20.cloned.1.call-start = ((), (), s32[]{:S(2)}) async-start(), calls=%async_computation.25 | async-start | bytes 4456448 | tf_op jit(solution)/shard_map/reduce_scatter | solution.py:348
  1355.6 733.3 %reduce-scatter.28.cloned.1.call-start = ((), (), s32[]{:S(2)}) async-start(), calls=%async_computation.29 | async-start | bytes 17825792 | tf_op jit(solution)/shard_map/reduce_scatter | solution.py:129
  1366.7 1073.3 %reduce-scatter.30.cloned.1.call-start = ((), (), s32[]{:S(2)}) async-start(), calls=%async_computation.30 | async-start | bytes 17825792 | tf_op jit(solution)/shard_map/reduce_scatter | solution.py:132
  1376.5 1414.8 %reduce-scatter.32.cloned.1.call-start = ((), (), s32[]{:S(2)}) async-start(), calls=%async_computation.31 | async-start | bytes 17825792 | tf_op jit(solution)/shard_map/reduce_scatter | solution.py:135
  (110 other events, 3264.8 us)
Sparse Core Ops, SparseCore 0:
  53.0 5.3 all-gather.12
  61.1 77.0 all-gather.14
  141.0 74.4 all-gather.16
  218.1 76.0 all-gather.18
  296.9 100.4 all-gather.20
  405.9 9.3 reduce-scatter.11
  449.8 6.2 all-gather.22
  459.2 293.3 all-gather.24
  754.8 8.4 all-gather.28
  766.3 315.7 all-gather.26
  1179.9 9.3 reduce-scatter.15
  1194.4 10.1 all-gather.30
  1326.1 6.8 reduce-scatter.17
  1338.5 6.8 reduce-scatter.13
  1347.5 100.1 reduce-scatter.25
  1449.9 94.6 reduce-scatter.23
  1546.7 94.6 reduce-scatter.21
  1643.5 94.6 reduce-scatter.19
  1740.5 348.3 reduce-scatter.27
  2091.0 348.9 reduce-scatter.29
  2442.3 348.9 reduce-scatter.31
